TPU v7x, 32 devices: a whole 2x2x4 slice. The times are simulated.
32 devices in a mesh: grp: 2 (over y), leaf: 16 (over z, x, core).
Axes of the slice: x: 2, y: 2, z: 4, core: 2. Of those that a mesh axis runs over, the one named last changes fastest.
Arguments:
- vectors: float32 [16, 32768], P(None, ('grp', 'leaf')), may hold values from -6 to 6
- points: float32 [3, 32768], P(None, ('grp', 'leaf')), may hold values from -1 to 2
- near_lists: int32 [64, 6], P(('grp', 'leaf')), may hold values from -1 to 5, as said below
- inter_lists: int32 [64, 16], P(('grp', 'leaf')), may hold values from 0 to 31, as said below
- skeleton: int32 [64, 64], P(('grp', 'leaf')), may hold values from 0 to 511, as said below
- interp: float32 [64, 64, 512], P(('grp', 'leaf')), may hold values from -0.25 to 0.25
- transfer: float32 [64, 64, 128], P(('grp', 'leaf')), may hold values from -0.125 to 0.125
- coarse_points: float32 [2, 3, 128], replicated, may hold values from 0 to 1
Outputs:
- filtered: float32 [16, 32768], P(None, ('grp', 'leaf'))
Inputs may be any that keep to these rules, and one draw needn't show every extreme that they name: `near_lists`: place w of leaf l's window is leaf (l // 2 - 1) * 2 + w. Slot 0 holds the leaf itself (2 + l % 2); the next slots hold distinct places of other leaves of the same subtree; then -1 to the end of the row. `inter_lists`: distinct leaves of the leaf's own subtree, numbered from the subtree's first leaf, none in the leaf's window. `skeleton`: distinct places within the leaf.
All inputs are finite; a program needn't handle non-finite values.
Results may differ from a plain program's by a relative error of at most 0.00013.
Values sent between devices are 32-bit elements; how exact they have to be, the bound alone decides.
No kernel may reach another device: no remote copies, remote signals or barrier semaphores. Data moves between devices by JAX's collectives and lax.ppermute only.
A program may use at most 64 MiB of HBM per device.

v0:
```python
import jax
import jax.numpy as jnp
from jax import lax
from jax.sharding import PartitionSpec as P

kappa_scale = 3.4641016151377544
centre = 0.05
half_width = 0.05
highest = lax.Precision.HIGHEST


def with_halo(x, sides, width):
    for axis, dim in sides:
        devices, length = (lax.axis_size(axis), x.shape[dim])
        up = [(i, (i + 1) % devices) for i in range(devices - 1)]
        down = [(j, i) for i, j in up]
        last = lax.slice_in_dim(x, length - width, length, axis=dim)
        initial = lax.slice_in_dim(x, 0, width, axis=dim)
        before = lax.ppermute(last, axis, up)
        after = lax.ppermute(initial, axis, down)
        x = jnp.concatenate([before, x, after], axis=dim)
    return x


def matern(source, target):
    delta_x = source[..., 0, :, None] - target[..., 0, None, :]
    delta_y = source[..., 1, :, None] - target[..., 1, None, :]
    delta_z = source[..., 2, :, None] - target[..., 2, None, :]
    scaled = kappa_scale * jnp.sqrt(delta_x * delta_x + delta_y * delta_y + delta_z * delta_z)
    return (1.0 + scaled) * jnp.exp(-scaled)


def on_device(vectors, points, near_lists, inter_lists, skeleton, interp, transfer, coarse_points):
    per_dev = near_lists.shape[0]
    slot_count = near_lists.shape[1]
    leaf_size = interp.shape[2]
    vec_count = vectors.shape[0]
    leaf_index = lax.axis_index("leaf")
    group_index = lax.axis_index("grp")
    group_count = lax.axis_size("grp")
    leaf_points = points.reshape(3, per_dev, leaf_size).transpose(1, 0, 2)
    skel_points = jnp.take_along_axis(leaf_points, skeleton[:, None, :], axis=2)
    subtree_skel = lax.all_gather(skel_points, "leaf", axis=0, tiled=True)
    own_coarse = lax.dynamic_index_in_dim(coarse_points, group_index, 0, keepdims=False)
    apart = (jnp.arange(group_count) != group_index).astype(jnp.float32)
    coupling = matern(coarse_points, own_coarse[None]) * apart[:, None, None]
    live_slots = jnp.max(jnp.sum((near_lists >= 0).astype(jnp.int32), axis=1))
    first_leaf = leaf_index * per_dev
    subtree_lists = lax.all_gather(inter_lists, "leaf", axis=0, tiled=True)
    own_ids = first_leaf + jnp.arange(per_dev, dtype=jnp.int32)
    hits = jnp.sum(
        (subtree_lists[:, :, None] == own_ids[None, None, :]).astype(jnp.float32), axis=1
    )
    push_kernel = matern(skel_points[None], subtree_skel[:, None]) * hits[:, :, None, None]

    def operate(field):
        stacked = jnp.concatenate([points, field], axis=0)
        window = with_halo(stacked, (("leaf", 1),), per_dev * leaf_size)
        window_points = window[:3].reshape(3, 3 * per_dev, leaf_size)
        window_vecs = window[3:].reshape(vec_count, 3 * per_dev, leaf_size)

        def near_slot(slot, running):
            chosen = lax.dynamic_index_in_dim(near_lists, slot, 1, keepdims=False)
            present = (chosen >= 0).astype(jnp.float32)
            safe_place = jnp.where(chosen >= 0, chosen, 0)
            source_points = jnp.take(window_points, safe_place, axis=1).transpose(1, 0, 2)
            source_vecs = jnp.take(window_vecs, safe_place, axis=1)
            kernel = matern(source_points, leaf_points)
            product = jnp.einsum("vlp,lpq->lvq", source_vecs, kernel, precision=highest)
            return running + present[:, None, None] * product

        near_part = lax.fori_loop(
            0, live_slots, near_slot, jnp.zeros((per_dev, vec_count, leaf_size), jnp.float32)
        )
        leaf_vecs = field.reshape(vec_count, per_dev, leaf_size)
        coeffs = jnp.einsum("vlp,lrp->lvr", leaf_vecs, interp, precision=highest)
        leaf_far = lax.psum_scatter(
            jnp.einsum("jvr,tjrq->tvq", coeffs, push_kernel, precision=highest),
            "leaf",
            scatter_dimension=0,
            tiled=True,
        )
        upward = jnp.einsum("lvr,lrc->vc", coeffs, transfer, precision=highest)
        subtree_total = lax.psum(upward, "leaf")
        group_coeffs = lax.all_gather(subtree_total[None], "grp", axis=0, tiled=True)
        coarse_field = jnp.einsum("avr,arq->vq", group_coeffs, coupling, precision=highest)
        downward = leaf_far + jnp.einsum("vc,lrc->lvr", coarse_field, transfer, precision=highest)
        far_part = jnp.einsum("lvr,lrp->lvp", downward, interp, precision=highest)
        combined = (near_part + far_part) / (leaf_size * slot_count)
        return combined.transpose(1, 0, 2).reshape(vec_count, per_dev * leaf_size)

    term_one = (operate(vectors) - centre * vectors) / half_width
    term_two = 2.0 * (operate(term_one) - centre * term_one) / half_width - vectors
    term_three = 2.0 * (operate(term_two) - centre * term_two) / half_width - term_one
    squares = lax.psum(jnp.sum(term_three * term_three, axis=1), ("grp", "leaf"))
    total_points = vectors.shape[1] * group_count * lax.axis_size("leaf")
    return term_three / jnp.sqrt(squares / total_points + 1e-06)[:, None]


def solution(mesh):
    placed = (
        P(None, ("grp", "leaf")),
        P(None, ("grp", "leaf")),
        P(("grp", "leaf"), None),
        P(("grp", "leaf"), None),
        P(("grp", "leaf"), None),
        P(("grp", "leaf"), None, None),
        P(("grp", "leaf"), None, None),
        P(),
    )
    return jax.shard_map(
        on_device, mesh=mesh, in_specs=placed, out_specs=P(None, ("grp", "leaf")), check_vma=False
    )
```

profile of v0, /device:TPU:10, one launch (start us, length us, event | category | flops | bytes accessed | tf_op | source)
XLA Modules:
  0.0 312.5 jit_solution(3287674258489741425)
XLA Ops:
  6.5 0.9 pad_maximum_fusion.3
  7.5 2.1 collective-permute-start.1
  9.5 2.4 collective-permute-start
  11.9 0.9 copy.61
  13.0 1.2 gather_fusion.6
  14.4 15.5 %all-gather = s32[16,2,16]{2,1,0:T(2,128)S(1)} all-gather(s32[1,2,16]{2,1,0:T(2,128)S(1)} %bitcast.260), channel_id=1, replica_groups=mesh['grp'=2,'leaf'=16] {'leaf'}, dimensions={0}, use_global_device_ids=true | all-gather | bytes 2176 | tf_op jit(solution)/shard_map/all_gather | solution.py:49
  30.1 21.1 %all_gather.15 = f32[32,3,64]{2,1,0:T(4,128)S(1)} all-gather(f32[2,3,64]{2,1,0:T(4,128)S(1)} %bitcast_select_fusion.1), channel_id=1, replica_groups=mesh['grp'=2,'leaf'=16] {'leaf'}, dimensions={0}, use_global_device_ids=true | all-gather | bytes 26112 | tf_op jit(solution)/shard_map/all_gather | solution.py:43
  51.6 3.5 %convolution_bitcast_fusion.2 = f32[32,16,64]{2,1,0:T(8,128)} fusion(f32[32,2]{1,0:T(8,128)S(1)} %copy.67, f32[32,64]{1,0:T(8,128)S(1)} %bitcast.254, f32[2,64]{1,0:T(2,128)S(1)} %bitcast.264, f32[32,64]{1,0:T(8,128)S(1)} %bitcast.257, f32[2,64]{1,0:T(2,128)S(1)} %bitcast.267, f32[32,64]{1,0:T(8,128)S(1)} %bitcast.251, f32[2,64]{1,0:T(2,128)S(1)} %bitcast.261, ...), kind=kOutput, calls=%fused_computation.145 | convolution fusion | flops 53739520 | bytes 165632 | tf_op jit(solution)/shard_map/jvr,tjrq->tvq/dot_general | solution.py:78
  56.1 24.3 %psum.28 = f32[1,16,128]{2,1,0:T(8,128)S(1)} all-reduce(f32[1,16,128]{2,1,0:T(8,128)S(1)} %convolution_bitcast_fusion.8), channel_id=1, replica_groups=mesh['grp'=2,'leaf'=16] {'leaf'}, use_global_device_ids=true, to_apply=%region_6.9 | all-reduce | flops 2048 | bytes 16384 | tf_op jit(solution)/shard_map/psum | solution.py:84
  80.4 4.4 %all_gather.17 = f32[2,16,128]{2,1,0:T(8,128)S(1)} all-gather(f32[1,16,128]{2,1,0:T(8,128)S(1)} %psum.28), channel_id=1, replica_groups=mesh['grp'=2,'leaf'=16] {'grp'}, dimensions={0}, use_global_device_ids=true | all-gather | bytes 24576 | tf_op jit(solution)/shard_map/all_gather | solution.py:85
  85.3 0.6 reduce_max.9
  86.1 28.6 %while.30 = (s32[]{:T(128)}, f32[2,16,512]{2,1,0:T(8,128)S(1)}, s32[]{:T(128)}, s32[2,6]{0,1:T(8,128)S(1)}, f32[16,6,512]{2,0,1:T(8,128)S(1)}, /*index=5*/f32[3,...) while((s32[]{:T(128)}, f32[2,16,512]{2,1,0:T(8,128)S(1)}, s32[]{:T(128)}, ...), condition=%wide.region_3.0_spmd, body=%wide.region_2.0_spmd.sunk | while | flops 107008024 | bytes 479441 | solution.py:72
  87.9 2.8 fusion.199
  92.6 2.8 fusion.199
  97.3 2.8 fusion.199
  102.0 2.8 fusion.199
  106.6 2.8 fusion.199
  111.3 2.8 fusion.199
  114.7 0.9 fusion.116
  116.0 1.9 collective-permute-start.3
  117.9 2.4 collective-permute-start.2
  120.7 3.5 %convolution_bitcast_fusion.1 = f32[32,16,64]{2,1,0:T(8,128)} fusion(f32[32,2]{1,0:T(8,128)S(1)} %copy.67, f32[32,64]{1,0:T(8,128)S(1)} %bitcast.255, f32[2,64]{1,0:T(2,128)S(1)} %bitcast.265, f32[32,64]{1,0:T(8,128)S(1)} %bitcast.258, f32[2,64]{1,0:T(2,128)S(1)} %bitcast.268, f32[32,64]{1,0:T(8,128)S(1)} %bitcast.252, f32[2,64]{1,0:T(2,128)S(1)} %bitcast.262, ...), kind=kOutput, calls=%fused_computation.144 | convolution fusion | flops 53739520 | bytes 165632 | tf_op jit(solution)/shard_map/jvr,tjrq->tvq/dot_general | solution.py:78
  124.4 26.7 %psum.29 = f32[1,16,128]{2,1,0:T(8,128)S(1)} all-reduce(f32[1,16,128]{2,1,0:T(8,128)S(1)} %convolution_bitcast_fusion.7), channel_id=1, replica_groups=mesh['grp'=2,'leaf'=16] {'leaf'}, use_global_device_ids=true, to_apply=%region_10.13 | all-reduce | flops 2048 | bytes 16384 | tf_op jit(solution)/shard_map/psum | solution.py:84
  151.2 4.4 %all_gather.18 = f32[2,16,128]{2,1,0:T(8,128)S(1)} all-gather(f32[1,16,128]{2,1,0:T(8,128)S(1)} %psum.29), channel_id=1, replica_groups=mesh['grp'=2,'leaf'=16] {'grp'}, dimensions={0}, use_global_device_ids=true | all-gather | bytes 24576 | tf_op jit(solution)/shard_map/all_gather | solution.py:85
  156.0 28.8 %while.31 = (s32[]{:T(128)}, f32[2,16,512]{2,1,0:T(8,128)S(1)}, s32[]{:T(128)}, s32[2,6]{0,1:T(8,128)S(1)}, f32[16,6,512]{2,0,1:T(8,128)S(1)}, /*index=5*/f32[3,...) while((s32[]{:T(128)}, f32[2,16,512]{2,1,0:T(8,128)S(1)}, s32[]{:T(128)}, ...), condition=%wide.region_8.11_spmd, body=%wide.region_7.10_spmd.sunk | while | flops 107008024 | bytes 479441 | solution.py:72
  158.1 2.8 fusion.203
  162.7 2.8 fusion.203
  167.4 2.8 fusion.203
  172.1 2.8 fusion.203
  176.8 2.8 fusion.203
  181.4 2.8 fusion.203
  185.3 0.9 fusion.115
  186.6 1.9 collective-permute-start.5
  188.5 2.4 collective-permute-start.4
  191.3 3.5 %convolution_bitcast_fusion = f32[32,16,64]{2,1,0:T(8,128)} fusion(f32[32,2]{1,0:T(8,128)S(1)} %copy.67, f32[32,64]{1,0:T(8,128)S(1)} %bitcast.256, f32[2,64]{1,0:T(2,128)S(1)} %bitcast.266, f32[32,64]{1,0:T(8,128)S(1)} %bitcast.259, f32[2,64]{1,0:T(2,128)S(1)} %bitcast.269, f32[32,64]{1,0:T(8,128)S(1)} %bitcast.253, f32[2,64]{1,0:T(2,128)S(1)} %bitcast.263, ...), kind=kOutput, calls=%fused_computation.143 | convolution fusion | flops 53739520 | bytes 165632 | tf_op jit(solution)/shard_map/jvr,tjrq->tvq/dot_general | solution.py:78
  195.0 28.1 %psum.30 = f32[1,16,128]{2,1,0:T(8,128)S(1)} all-reduce(f32[1,16,128]{2,1,0:T(8,128)S(1)} %convolution_bitcast_fusion.6), channel_id=1, replica_groups=mesh['grp'=2,'leaf'=16] {'leaf'}, use_global_device_ids=true, to_apply=%region_14.17 | all-reduce | flops 2048 | bytes 16384 | tf_op jit(solution)/shard_map/psum | solution.py:84
  223.1 4.4 %all_gather.19 = f32[2,16,128]{2,1,0:T(8,128)S(1)} all-gather(f32[1,16,128]{2,1,0:T(8,128)S(1)} %psum.30), channel_id=1, replica_groups=mesh['grp'=2,'leaf'=16] {'grp'}, dimensions={0}, use_global_device_ids=true | all-gather | bytes 24576 | tf_op jit(solution)/shard_map/all_gather | solution.py:85
  227.9 28.6 %while.32 = (s32[]{:T(128)}, f32[2,16,512]{2,1,0:T(8,128)S(1)}, s32[]{:T(128)}, s32[2,6]{0,1:T(8,128)S(1)}, f32[16,6,512]{2,0,1:T(8,128)S(1)}, /*index=5*/f32[3,...) while((s32[]{:T(128)}, f32[2,16,512]{2,1,0:T(8,128)S(1)}, s32[]{:T(128)}, ...), condition=%wide.region_12.15_spmd, body=%wide.region_11.14_spmd.sunk | while | flops 107008024 | bytes 479441 | solution.py:72
  229.8 2.8 fusion.207
  234.5 2.8 fusion.207
  239.2 2.8 fusion.207
  243.8 2.8 fusion.207
  248.5 2.8 fusion.207
  253.2 2.8 fusion.207
  256.6 0.7 reduce-scatter.8.cloned.1.call-done
  257.3 0.9 fusion.114
  258.7 46.5 %psum.31 = f32[16]{0:T(128)S(1)} all-reduce(f32[16]{0:T(128)S(1)} %multiply_reduce_fusion), channel_id=1, replica_groups=mesh['grp'=2,'leaf'=16] {'grp','leaf'}, use_global_device_ids=true, to_apply=%region_16.19 | all-reduce | flops 16 | bytes 128 | tf_op jit(solution)/shard_map/psum | solution.py:95
  305.2 0.7 broadcast_divide_fusion
  (228 shorter events, 28.3 us)
Async XLA Ops:
  6.5 44.8 %copy-start = (f32[2,64,512]{2,1,0:T(8,128)S(1)}, f32[2,64,512]{2,1,0:T(8,128)}, u32[]{:S(2)}) copy-start(f32[2,64,512]{2,1,0:T(8,128)} %param.23) | copy-start | bytes 786436
  6.5 6.4 %copy-start.7 = (s32[2,64]{1,0:T(2,128)S(1)}, s32[2,64]{1,0:T(2,128)}, u32[]{:S(2)}) copy-start(s32[2,64]{1,0:T(2,128)} %param.22) | copy-start | bytes 1540
  6.5 7.8 %copy-start.5 = (s32[2,16]{1,0:T(2,128)S(1)}, s32[2,16]{1,0:T(2,128)}, u32[]{:S(2)}) copy-start(s32[2,16]{1,0:T(2,128)} %param.21) | copy-start | bytes 388
  6.5 108.2 %reduce-scatter.4.cloned.1.call-start = ((), (), s32[]{:S(2)}) async-start(), calls=%async_computation.3 | async-start | bytes 278528 | tf_op jit(solution)/shard_map/reduce_scatter | solution.py:77
  7.5 43.8 %copy-start.2 = (f32[16,1024]{1,0:T(8,128)S(1)}, f32[16,1024]{1,0:T(8,128)}, u32[]{:S(2)}) copy-start(f32[16,1024]{1,0:T(8,128)} %param.18) | copy-start | bytes 196612
  7.5 78.5 %collective-permute-start.1 = (f32[19,1024]{1,0:T(8,128)S(1)}, f32[19,1024]{1,0:T(8,128)S(1)}, u32[]{:S(2)}, u32[]{:S(2)}) collective-permute-start(f32[19,1024]{1,0:T(8,128)S(1)} %pad_maximum_fusion.3), channel_id=1, source_target_pairs={{1,0},{2,1},{3,2},{4,3},{5,4},{6,5},{7,6},{8,7},{9,8},{10,9},{11,1... | collective-permute-start | bytes 233480 | tf_op jit(solution)/shard_map/ppermute | solution.py:20
  9.5 76.4 %collective-permute-start = (f32[19,1024]{1,0:T(8,128)S(1)}, f32[19,1024]{1,0:T(8,128)S(1)}, u32[]{:S(2)}, u32[]{:S(2)}) collective-permute-start(f32[19,1024]{1,0:T(8,128)S(1)} %pad_maximum_fusion.3), channel_id=1, source_target_pairs={{0,1},{1,2},{2,3},{3,4},{4,5},{5,6},{6,7},{7,8},{8,9},{9,10},{10,1... | collective-permute-start | bytes 233480 | tf_op jit(solution)/shard_map/ppermute | solution.py:19
  55.1 0.7 copy-start.6
  55.1 0.9 copy-start.1
  55.1 29.7 %copy-start.4 = (f32[2,3,128]{2,0,1:T(2,128)S(1)}, f32[2,3,128]{2,0,1:T(2,128)}, u32[]{:S(2)}) copy-start(f32[2,3,128]{2,0,1:T(2,128)} %param.25) | copy-start | bytes 9220
  55.1 30.8 %copy-start.3 = (f32[3,1024]{1,0:T(4,128)S(1)}, f32[3,1024]{1,0:T(4,128)}, u32[]{:S(2)}) copy-start(f32[3,1024]{1,0:T(4,128)} %param.19) | copy-start | bytes 36868
  55.1 130.2 %reduce-scatter.6.cloned.1.call-start = ((), (), s32[]{:S(2)}) async-start(), calls=%async_computation.4 | async-start | bytes 278528 | tf_op jit(solution)/shard_map/reduce_scatter | solution.py:77
  116.0 39.9 %collective-permute-start.3 = (f32[19,1024]{1,0:T(8,128)S(1)}, f32[19,1024]{1,0:T(8,128)S(1)}, u32[]{:S(2)}, u32[]{:S(2)}) collective-permute-start(f32[19,1024]{1,0:T(8,128)S(1)} %pad_maximum_fusion.4), channel_id=1, source_target_pairs={{1,0},{2,1},{3,2},{4,3},{5,4},{6,5},{7,6},{8,7},{9,8},{10,9},{11,1... | collective-permute-start | bytes 233480 | tf_op jit(solution)/shard_map/ppermute | solution.py:20
  117.9 38.0 %collective-permute-start.2 = (f32[19,1024]{1,0:T(8,128)S(1)}, f32[19,1024]{1,0:T(8,128)S(1)}, u32[]{:S(2)}, u32[]{:S(2)}) collective-permute-start(f32[19,1024]{1,0:T(8,128)S(1)} %pad_maximum_fusion.4), channel_id=1, source_target_pairs={{0,1},{1,2},{2,3},{3,4},{4,5},{5,6},{6,7},{7,8},{8,9},{9,10},{10,1... | collective-permute-start | bytes 233480 | tf_op jit(solution)/shard_map/ppermute | solution.py:19
  124.4 132.9 %reduce-scatter.8.cloned.1.call-start = ((), (), s32[]{:S(2)}) async-start(), calls=%async_computation.5 | async-start | bytes 278528 | tf_op jit(solution)/shard_map/reduce_scatter | solution.py:77
  186.6 41.2 %collective-permute-start.5 = (f32[19,1024]{1,0:T(8,128)S(1)}, f32[19,1024]{1,0:T(8,128)S(1)}, u32[]{:S(2)}, u32[]{:S(2)}) collective-permute-start(f32[19,1024]{1,0:T(8,128)S(1)} %pad_maximum_fusion.5), channel_id=1, source_target_pairs={{1,0},{2,1},{3,2},{4,3},{5,4},{6,5},{7,6},{8,7},{9,8},{10,9},{11,1... | collective-permute-start | bytes 233480 | tf_op jit(solution)/shard_map/ppermute | solution.py:20
  188.5 39.3 %collective-permute-start.4 = (f32[19,1024]{1,0:T(8,128)S(1)}, f32[19,1024]{1,0:T(8,128)S(1)}, u32[]{:S(2)}, u32[]{:S(2)}) collective-permute-start(f32[19,1024]{1,0:T(8,128)S(1)} %pad_maximum_fusion.5), channel_id=1, source_target_pairs={{0,1},{1,2},{2,3},{3,4},{4,5},{5,6},{6,7},{7,8},{8,9},{9,10},{10,1... | collective-permute-start | bytes 233480 | tf_op jit(solution)/shard_map/ppermute | solution.py:19
Sparse Core Ops, SparseCore 0:
  55.2 56.6 reduce-scatter.3
  124.5 60.7 reduce-scatter.5
  195.1 62.1 reduce-scatter.7
where the time goes:
time: 313 us; the launch traced here: 312 us
  blocking collectives  175 us (56%)
  matrix products  66.6 us (21%)
  local copies, waits for them, and re-layouts  24.2 us (8%)
  loops' own time  13.7 us (4%)
  between operations  13.7 us (4%)
  starting transfers between devices  13.2 us (4%)
  other arithmetic  4.5 us (1%)
    psum x3, blocking collectives, operate(): subtree_total = lax.psum(upward, 'leaf')  79.1 us
    dot_general x18, matrix products, near_slot(): product = jnp.einsum('vlp,lpq->lvq', source_vecs, kernel, precision=highest)  50 us
    psum x1, blocking collectives, on_device(): lax.psum(jnp.sum(term_three * term_three, axis=1), ('grp', 'leaf'))  46.5 us
    all_gather x1, blocking collectives, on_device(): subtree_skel = lax.all_gather(skel_points, 'leaf', axis=0, tiled=True)  21.1 us
    all_gather x1, blocking collectives, on_device(): subtree_lists = lax.all_gather(inter_lists, 'leaf', axis=0, tiled=True)  15.5 us
    another operation x3, loops' own time, operate(): lax.fori_loop(0, live_slots, near_slot, jnp.zeros((per_dev, vec_count, le...  13.7 us
    all_gather x3, blocking collectives, operate(): lax.all_gather(subtree_total[None], 'grp', axis=0, tiled=True)  13.1 us
    dot_general x3, matrix products, operate(): jnp.einsum('jvr,tjrq->tvq', coeffs, push_kernel, precision=highest)  10.4 us
  transfers between devices with their start and end apart: 9, of which 2 were waited for; matrix products, arithmetic and copies ran while one was open for 29% of the time, Pallas kernels for 0%

commit v1 on v0

--- a/solution.py
+++ b/solution.py
@@ -7,6 +7,15 @@
 centre = 0.05
 half_width = 0.05
 highest = lax.Precision.HIGHEST
+
+
+def add_in_pairs(x, name):
+    devices = lax.axis_size(name)
+    result, far = (x, 1)
+    while far < devices:
+        result = result + lax.ppermute(result, name, [(i, i ^ far) for i in range(devices)])
+        far = 2 * far
+    return result
 
 
 def with_halo(x, sides, width):
@@ -81,7 +90,7 @@
             tiled=True,
         )
         upward = jnp.einsum("lvr,lrc->vc", coeffs, transfer, precision=highest)
-        subtree_total = lax.psum(upward, "leaf")
+        subtree_total = add_in_pairs(upward, "leaf")
         group_coeffs = lax.all_gather(subtree_total[None], "grp", axis=0, tiled=True)
         coarse_field = jnp.einsum("avr,arq->vq", group_coeffs, coupling, precision=highest)
         downward = leaf_far + jnp.einsum("vc,lrc->lvr", coarse_field, transfer, precision=highest)

time: 313 us -> 309 us (0.987)
  blocking collectives: 175 us -> 89.7 us
  waiting for transfers between devices: 1.34 us -> 69.5 us
  starting transfers between devices: 13.2 us -> 23.6 us
    psum x3 -> x0, blocking collectives: 79.1 us -> none  [operate(): subtree_total = lax.psum(upward, 'leaf')]
    reduce_scatter x3, waiting for transfers between devices: 1.24 us -> 52.9 us  [operate(): lax.psum_scatter(jnp.einsum('jvr,tjrq->tvq', coeffs, push_kernel, precisi...]
    ppermute x0 -> x12, waiting for transfers between devices: none -> 16.6 us  [add_in_pairs(): lax.ppermute(result, name, [(i, i ^ far) for i in range(devices)])]
    ppermute x0 -> x12, starting transfers between devices: none -> 10.4 us  [add_in_pairs(): lax.ppermute(result, name, [(i, i ^ far) for i in range(devices)])]
    psum x1, blocking collectives: 46.5 us -> 40 us  [on_device(): lax.psum(jnp.sum(term_three * term_three, axis=1), ('grp', 'leaf'))]
  transfers between devices with their start and end apart: 9 -> 21, of which waited for: 2 -> 11; matrix products, arithmetic and copies ran while one was open for 29% -> 29% of each run, Pallas kernels for 0% -> 0%
where the time goes in v1:
time: 309 us; the launch traced here: 306 us
  blocking collectives  89.7 us (29%)
  waiting for transfers between devices  69.5 us (22%)
  matrix products  66.6 us (22%)
  local copies, waits for them, and re-layouts  23.7 us (8%)
  starting transfers between devices  23.6 us (8%)
  loops' own time  14.9 us (5%)
  between operations  13.8 us (4%)
  other arithmetic  4.6 us (1%)
    reduce_scatter x3, waiting for transfers between devices, operate(): lax.psum_scatter(jnp.einsum('jvr,tjrq->tvq', coeffs, push_kernel, precisi...  52.9 us
    dot_general x18, matrix products, near_slot(): product = jnp.einsum('vlp,lpq->lvq', source_vecs, kernel, precision=highest)  50 us
    psum x1, blocking collectives, on_device(): lax.psum(jnp.sum(term_three * term_three, axis=1), ('grp', 'leaf'))  40 us
    all_gather x1, blocking collectives, on_device(): subtree_skel = lax.all_gather(skel_points, 'leaf', axis=0, tiled=True)  21.1 us
    ppermute x12, waiting for transfers between devices, add_in_pairs(): lax.ppermute(result, name, [(i, i ^ far) for i in range(devices)])  16.6 us
    all_gather x1, blocking collectives, on_device(): subtree_lists = lax.all_gather(inter_lists, 'leaf', axis=0, tiled=True)  15.5 us
    another operation x3, loops' own time, operate(): lax.fori_loop(0, live_slots, near_slot, jnp.zeros((per_dev, vec_count, le...  14.9 us
    all_gather x3, blocking collectives, operate(): lax.all_gather(subtree_total[None], 'grp', axis=0, tiled=True)  13.1 us
  transfers between devices with their start and end apart: 21, of which 11 were waited for; matrix products, arithmetic and copies ran while one was open for 29% of the time, Pallas kernels for 0%

profile of v1, /device:TPU:10, one launch (start us, length us, event | category | flops | bytes accessed | tf_op | source)
XLA Modules:
  0.0 306.4 jit_solution(5130244202178165832)
XLA Ops:
  7.5 2.1 collective-permute-start.1
  9.5 2.4 collective-permute-start
  13.0 1.2 gather_fusion.6
  14.4 15.5 %all-gather.3 = s32[16,2,16]{2,1,0:T(2,128)S(1)} all-gather(s32[1,2,16]{2,1,0:T(2,128)S(1)} %bitcast.263), channel_id=1, replica_groups=mesh['grp'=2,'leaf'=16] {'leaf'}, dimensions={0}, use_global_device_ids=true | all-gather | bytes 2176 | tf_op jit(solution)/shard_map/all_gather | solution.py:58
  30.1 21.1 %all_gather.15 = f32[32,3,64]{2,1,0:T(4,128)S(1)} all-gather(f32[2,3,64]{2,1,0:T(4,128)S(1)} %bitcast_select_fusion.1), channel_id=1, replica_groups=mesh['grp'=2,'leaf'=16] {'leaf'}, dimensions={0}, use_global_device_ids=true | all-gather | bytes 26112 | tf_op jit(solution)/shard_map/all_gather | solution.py:52
  51.6 3.5 %convolution_bitcast_fusion.2 = f32[32,16,64]{2,1,0:T(8,128)} fusion(f32[32,2]{1,0:T(8,128)S(1)} %copy.67, f32[32,64]{1,0:T(8,128)S(1)} %bitcast.257, f32[2,64]{1,0:T(2,128)S(1)} %bitcast.267, f32[32,64]{1,0:T(8,128)S(1)} %bitcast.260, f32[2,64]{1,0:T(2,128)S(1)} %bitcast.270, f32[32,64]{1,0:T(8,128)S(1)} %bitcast.254, f32[2,64]{1,0:T(2,128)S(1)} %bitcast.264, ...), kind=kOutput, calls=%fused_computation.145 | convolution fusion | flops 53739520 | bytes 165632 | tf_op jit(solution)/shard_map/jvr,tjrq->tvq/dot_general | solution.py:87
  57.0 3.2 %collective-permute-done.3 = f32[16,128]{1,0:T(8,128)S(1)} collective-permute-done((f32[16,128]{1,0:T(8,128)S(1)}, f32[16,128]{1,0:T(8,128)S(1)}, u32[]{:S(2)}, u32[]{:S(2)}) %collective-permute-start.3) | collective-permute-done | bytes 8224 | tf_op jit(solution)/shard_map/ppermute | solution.py:16
  60.2 3.3 %collective-permute-start.4 = (f32[16,128]{1,0:T(8,128)S(1)}, f32[16,128]{1,0:T(8,128)S(1)}, u32[]{:S(2)}, u32[]{:S(2)}) collective-permute-start(f32[16,128]{1,0:T(8,128)S(1)} %add.182), channel_id=1, source_target_pairs={{0,4},{1,5},{2,6},{3,7},{4,0},{5,1},{6,2},{7,3},{8,12},{9,13},{10,... | collective-permute-start | bytes 24584 | tf_op jit(solution)/shard_map/ppermute | solution.py:16
  63.5 1.6 collective-permute-done.4
  67.2 2.4 collective-permute-done.5
  69.7 4.3 %all-gather = f32[32,128]{1,0:T(8,128)S(1)} all-gather(f32[16,128]{1,0:T(8,128)S(1)} %add.184), channel_id=2, replica_groups=mesh['grp'=2,'leaf'=16] {'grp'}, dimensions={0}, use_global_device_ids=true | all-gather | bytes 24576 | tf_op jit(solution)/shard_map/all_gather | solution.py:94
  74.5 29.0 %while.30 = (s32[]{:T(128)}, f32[2,16,512]{2,1,0:T(8,128)S(1)}, s32[]{:T(128)}, s32[2,6]{0,1:T(8,128)S(1)}, f32[16,6,512]{2,0,1:T(8,128)S(1)}, /*index=5*/f32[3,...) while((s32[]{:T(128)}, f32[2,16,512]{2,1,0:T(8,128)S(1)}, s32[]{:T(128)}, ...), condition=%wide.region_3.0_spmd, body=%wide.region_2.0_spmd.sunk | while | flops 107008024 | bytes 479441 | solution.py:81
  76.5 2.8 fusion.199
  81.2 2.8 fusion.199
  85.9 2.8 fusion.199
  90.7 2.8 fusion.199
  95.4 2.8 fusion.199
  100.1 2.8 fusion.199
  103.6 8.4 %reduce-scatter.4.cloned.1.call-done = f32[2,16,64]{2,1,0:T(8,128)} async-done(((f32[32,16,64]{2,1,0:T(8,128)}), f32[2,16,64]{2,1,0:T(8,128)}) %reduce-scatter.4.cloned.1.call-update) | async-done | bytes 8208 | tf_op jit(solution)/shard_map/reduce_scatter | solution.py:86
  115.5 3.1 %collective-permute-done.9 = f32[16,128]{1,0:T(8,128)S(1)} collective-permute-done((f32[16,128]{1,0:T(8,128)S(1)}, f32[16,128]{1,0:T(8,128)S(1)}, u32[]{:S(2)}, u32[]{:S(2)}) %collective-permute-start.9) | collective-permute-done | bytes 8224 | tf_op jit(solution)/shard_map/ppermute | solution.py:16
  119.1 1.9 collective-permute-start.7
  121.1 2.4 collective-permute-start.6
  123.5 1.6 collective-permute-start.11
  125.1 3.4 %convolution_bitcast_fusion.1 = f32[32,16,64]{2,1,0:T(8,128)} fusion(f32[32,2]{1,0:T(8,128)S(1)} %copy.67, f32[32,64]{1,0:T(8,128)S(1)} %bitcast.258, f32[2,64]{1,0:T(2,128)S(1)} %bitcast.268, f32[32,64]{1,0:T(8,128)S(1)} %bitcast.261, f32[2,64]{1,0:T(2,128)S(1)} %bitcast.271, f32[32,64]{1,0:T(8,128)S(1)} %bitcast.255, f32[2,64]{1,0:T(2,128)S(1)} %bitcast.265, ...), kind=kOutput, calls=%fused_computation.144 | convolution fusion | flops 53739520 | bytes 165632 | tf_op jit(solution)/shard_map/jvr,tjrq->tvq/dot_general | solution.py:87
  128.6 4.4 %all-gather.1 = f32[32,128]{1,0:T(8,128)S(1)} all-gather(f32[16,128]{1,0:T(8,128)S(1)} %add.195), channel_id=3, replica_groups=mesh['grp'=2,'leaf'=16] {'grp'}, dimensions={0}, use_global_device_ids=true | all-gather | bytes 24576 | tf_op jit(solution)/shard_map/all_gather | solution.py:94
  133.5 29.2 %while.31 = (s32[]{:T(128)}, f32[2,16,512]{2,1,0:T(8,128)S(1)}, s32[]{:T(128)}, s32[2,6]{0,1:T(8,128)S(1)}, f32[16,6,512]{2,0,1:T(8,128)S(1)}, /*index=5*/f32[3,...) while((s32[]{:T(128)}, f32[2,16,512]{2,1,0:T(8,128)S(1)}, s32[]{:T(128)}, ...), condition=%wide.region_7.10_spmd, body=%wide.region_6.9_spmd.sunk | while | flops 107008024 | bytes 479441 | solution.py:81
  135.6 2.8 fusion.203
  140.3 2.8 fusion.203
  145.1 2.8 fusion.203
  149.8 2.8 fusion.203
  154.5 2.8 fusion.203
  159.3 2.8 fusion.203
  162.7 22.2 %reduce-scatter.6.cloned.1.call-done = f32[2,16,64]{2,1,0:T(8,128)} async-done(((f32[32,16,64]{2,1,0:T(8,128)}), f32[2,16,64]{2,1,0:T(8,128)}) %reduce-scatter.6.cloned.1.call-update) | async-done | bytes 8208 | tf_op jit(solution)/shard_map/reduce_scatter | solution.py:86
  188.4 3.1 %collective-permute-done.15 = f32[16,128]{1,0:T(8,128)S(1)} collective-permute-done((f32[16,128]{1,0:T(8,128)S(1)}, f32[16,128]{1,0:T(8,128)S(1)}, u32[]{:S(2)}, u32[]{:S(2)}) %collective-permute-start.15) | collective-permute-done | bytes 8224 | tf_op jit(solution)/shard_map/ppermute | solution.py:16
  192.1 1.9 collective-permute-start.13
  194.0 2.4 collective-permute-start.12
  196.5 1.6 collective-permute-start.17
  198.0 3.4 %convolution_bitcast_fusion = f32[32,16,64]{2,1,0:T(8,128)} fusion(f32[32,2]{1,0:T(8,128)S(1)} %copy.67, f32[32,64]{1,0:T(8,128)S(1)} %bitcast.259, f32[2,64]{1,0:T(2,128)S(1)} %bitcast.269, f32[32,64]{1,0:T(8,128)S(1)} %bitcast.262, f32[2,64]{1,0:T(2,128)S(1)} %bitcast.272, f32[32,64]{1,0:T(8,128)S(1)} %bitcast.256, f32[2,64]{1,0:T(2,128)S(1)} %bitcast.266, ...), kind=kOutput, calls=%fused_computation.143 | convolution fusion | flops 53739520 | bytes 165632 | tf_op jit(solution)/shard_map/jvr,tjrq->tvq/dot_general | solution.py:87
  201.5 4.4 %all-gather.2 = f32[32,128]{1,0:T(8,128)S(1)} all-gather(f32[16,128]{1,0:T(8,128)S(1)} %add.201), channel_id=4, replica_groups=mesh['grp'=2,'leaf'=16] {'grp'}, dimensions={0}, use_global_device_ids=true | all-gather | bytes 24576 | tf_op jit(solution)/shard_map/all_gather | solution.py:94
  206.4 29.0 %while.32 = (s32[]{:T(128)}, f32[2,16,512]{2,1,0:T(8,128)S(1)}, s32[]{:T(128)}, s32[2,6]{0,1:T(8,128)S(1)}, f32[16,6,512]{2,0,1:T(8,128)S(1)}, /*index=5*/f32[3,...) while((s32[]{:T(128)}, f32[2,16,512]{2,1,0:T(8,128)S(1)}, s32[]{:T(128)}, ...), condition=%wide.region_10.13_spmd, body=%wide.region_9.12_spmd.sunk | while | flops 107008024 | bytes 479441 | solution.py:81
  208.3 2.8 fusion.207
  213.0 2.8 fusion.207
  217.8 2.8 fusion.207
  222.5 2.8 fusion.207
  227.3 2.8 fusion.207
  232.0 2.8 fusion.207
  235.4 22.3 %reduce-scatter.8.cloned.1.call-done = f32[2,16,64]{2,1,0:T(8,128)} async-done(((f32[32,16,64]{2,1,0:T(8,128)}), f32[2,16,64]{2,1,0:T(8,128)}) %reduce-scatter.8.cloned.1.call-update) | async-done | bytes 8208 | tf_op jit(solution)/shard_map/reduce_scatter | solution.py:86
  259.1 40.0 %psum.7 = f32[16]{0:T(128)S(1)} all-reduce(f32[16]{0:T(128)S(1)} %multiply_reduce_fusion), channel_id=1, replica_groups=mesh['grp'=2,'leaf'=16] {'grp','leaf'}, use_global_device_ids=true, to_apply=%region_13.16 | all-reduce | flops 16 | bytes 128 | tf_op jit(solution)/shard_map/psum | solution.py:104
  (261 shorter events, 40.6 us)
Async XLA Ops:
  6.5 44.8 %copy-start = (f32[2,64,512]{2,1,0:T(8,128)S(1)}, f32[2,64,512]{2,1,0:T(8,128)}, u32[]{:S(2)}) copy-start(f32[2,64,512]{2,1,0:T(8,128)} %param.23) | copy-start | bytes 786436
  6.5 6.4 %copy-start.7 = (s32[2,64]{1,0:T(2,128)S(1)}, s32[2,64]{1,0:T(2,128)}, u32[]{:S(2)}) copy-start(s32[2,64]{1,0:T(2,128)} %param.22) | copy-start | bytes 1540
  6.5 7.8 %copy-start.5 = (s32[2,16]{1,0:T(2,128)S(1)}, s32[2,16]{1,0:T(2,128)}, u32[]{:S(2)}) copy-start(s32[2,16]{1,0:T(2,128)} %param.21) | copy-start | bytes 388
  6.5 105.4 %reduce-scatter.4.cloned.1.call-start = ((), (), s32[]{:S(2)}) async-start(), calls=%async_computation.3 | async-start | bytes 278528 | tf_op jit(solution)/shard_map/reduce_scatter | solution.py:86
  7.5 43.8 %copy-start.2 = (f32[16,1024]{1,0:T(8,128)S(1)}, f32[16,1024]{1,0:T(8,128)}, u32[]{:S(2)}) copy-start(f32[16,1024]{1,0:T(8,128)} %param.18) | copy-start | bytes 196612
  7.5 66.9 %collective-permute-start.1 = (f32[19,1024]{1,0:T(8,128)S(1)}, f32[19,1024]{1,0:T(8,128)S(1)}, u32[]{:S(2)}, u32[]{:S(2)}) collective-permute-start(f32[19,1024]{1,0:T(8,128)S(1)} %pad_maximum_fusion.3), channel_id=1, source_target_pairs={{1,0},{2,1},{3,2},{4,3},{5,4},{6,5},{7,6},{8,7},{9,8},{10,9},{11,1... | collective-permute-start | bytes 233480 | tf_op jit(solution)/shard_map/ppermute | solution.py:29
  9.5 64.9 %collective-permute-start = (f32[19,1024]{1,0:T(8,128)S(1)}, f32[19,1024]{1,0:T(8,128)S(1)}, u32[]{:S(2)}, u32[]{:S(2)}) collective-permute-start(f32[19,1024]{1,0:T(8,128)S(1)} %pad_maximum_fusion.3), channel_id=1, source_target_pairs={{0,1},{1,2},{2,3},{3,4},{4,5},{5,6},{6,7},{7,8},{8,9},{9,10},{10,1... | collective-permute-start | bytes 233480 | tf_op jit(solution)/shard_map/ppermute | solution.py:28
  51.6 3.6 %copy-start.1 = (f32[2,64,128]{2,1,0:T(8,128)S(1)}, f32[2,64,128]{2,1,0:T(8,128)}, u32[]{:S(2)}) copy-start(f32[2,64,128]{2,1,0:T(8,128)} %param.24) | copy-start | bytes 196612
  51.6 4.1 %copy-start.4 = (f32[2,3,128]{2,0,1:T(2,128)S(1)}, f32[2,3,128]{2,0,1:T(2,128)}, u32[]{:S(2)}) copy-start(f32[2,3,128]{2,0,1:T(2,128)} %param.25) | copy-start | bytes 9220
  51.6 5.3 %copy-start.6 = (s32[2,6]{1,0:T(2,128)S(1)}, s32[2,6]{1,0:T(2,128)}, u32[]{:S(2)}) copy-start(s32[2,6]{1,0:T(2,128)} %param.20) | copy-start | bytes 148
  55.1 129.7 %reduce-scatter.6.cloned.1.call-start = ((), (), s32[]{:S(2)}) async-start(), calls=%async_computation.4 | async-start | bytes 278528 | tf_op jit(solution)/shard_map/reduce_scatter | solution.py:86
  55.4 1.2 collective-permute-start.2
  56.6 3.7 %collective-permute-start.3 = (f32[16,128]{1,0:T(8,128)S(1)}, f32[16,128]{1,0:T(8,128)S(1)}, u32[]{:S(2)}, u32[]{:S(2)}) collective-permute-start(f32[16,128]{1,0:T(8,128)S(1)} %add.181), channel_id=1, source_target_pairs={{0,2},{1,3},{2,0},{3,1},{4,6},{5,7},{6,4},{7,5},{8,10},{9,11},{10,... | collective-permute-start | bytes 24584 | tf_op jit(solution)/shard_map/ppermute | solution.py:16
  60.2 4.9 %collective-permute-start.4 = (f32[16,128]{1,0:T(8,128)S(1)}, f32[16,128]{1,0:T(8,128)S(1)}, u32[]{:S(2)}, u32[]{:S(2)}) collective-permute-start(f32[16,128]{1,0:T(8,128)S(1)} %add.182), channel_id=1, source_target_pairs={{0,4},{1,5},{2,6},{3,7},{4,0},{5,1},{6,2},{7,3},{8,12},{9,13},{10,... | collective-permute-start | bytes 24584 | tf_op jit(solution)/shard_map/ppermute | solution.py:16
  65.1 4.5 %collective-permute-start.5 = (f32[16,128]{1,0:T(8,128)S(1)}, f32[16,128]{1,0:T(8,128)S(1)}, u32[]{:S(2)}, u32[]{:S(2)}) collective-permute-start(f32[16,128]{1,0:T(8,128)S(1)} %add.183), channel_id=1, source_target_pairs={{0,8},{1,9},{2,10},{3,11},{4,12},{5,13},{6,14},{7,15},{8,0},{9,1},... | collective-permute-start | bytes 24584 | tf_op jit(solution)/shard_map/ppermute | solution.py:16
  66.3 8.1 %copy-start.3 = (f32[3,1024]{1,0:T(4,128)S(1)}, f32[3,1024]{1,0:T(4,128)}, u32[]{:S(2)}) copy-start(f32[3,1024]{1,0:T(4,128)} %param.19) | copy-start | bytes 36868
  113.8 1.2 collective-permute-start.8
  114.9 3.7 %collective-permute-start.9 = (f32[16,128]{1,0:T(8,128)S(1)}, f32[16,128]{1,0:T(8,128)S(1)}, u32[]{:S(2)}, u32[]{:S(2)}) collective-permute-start(f32[16,128]{1,0:T(8,128)S(1)} %add.192), channel_id=1, source_target_pairs={{0,2},{1,3},{2,0},{3,1},{4,6},{5,7},{6,4},{7,5},{8,10},{9,11},{10,... | collective-permute-start | bytes 24584 | tf_op jit(solution)/shard_map/ppermute | solution.py:16
  118.6 4.9 %collective-permute-start.10 = (f32[16,128]{1,0:T(8,128)S(1)}, f32[16,128]{1,0:T(8,128)S(1)}, u32[]{:S(2)}, u32[]{:S(2)}) collective-permute-start(f32[16,128]{1,0:T(8,128)S(1)} %add.193), channel_id=1, source_target_pairs={{0,4},{1,5},{2,6},{3,7},{4,0},{5,1},{6,2},{7,3},{8,12},{9,13},{10,... | collective-permute-start | bytes 24584 | tf_op jit(solution)/shard_map/ppermute | solution.py:16
  119.1 14.2 %collective-permute-start.7 = (f32[19,1024]{1,0:T(8,128)S(1)}, f32[19,1024]{1,0:T(8,128)S(1)}, u32[]{:S(2)}, u32[]{:S(2)}) collective-permute-start(f32[19,1024]{1,0:T(8,128)S(1)} %pad_maximum_fusion.4), channel_id=1, source_target_pairs={{1,0},{2,1},{3,2},{4,3},{5,4},{6,5},{7,6},{8,7},{9,8},{10,9},{11,1... | collective-permute-start | bytes 233480 | tf_op jit(solution)/shard_map/ppermute | solution.py:29
  121.1 12.3 %collective-permute-start.6 = (f32[19,1024]{1,0:T(8,128)S(1)}, f32[19,1024]{1,0:T(8,128)S(1)}, u32[]{:S(2)}, u32[]{:S(2)}) collective-permute-start(f32[19,1024]{1,0:T(8,128)S(1)} %pad_maximum_fusion.4), channel_id=1, source_target_pairs={{0,1},{1,2},{2,3},{3,4},{4,5},{5,6},{6,7},{7,8},{8,9},{9,10},{10,1... | collective-permute-start | bytes 233480 | tf_op jit(solution)/shard_map/ppermute | solution.py:28
  123.5 5.1 %collective-permute-start.11 = (f32[16,128]{1,0:T(8,128)S(1)}, f32[16,128]{1,0:T(8,128)S(1)}, u32[]{:S(2)}, u32[]{:S(2)}) collective-permute-start(f32[16,128]{1,0:T(8,128)S(1)} %add.194), channel_id=1, source_target_pairs={{0,8},{1,9},{2,10},{3,11},{4,12},{5,13},{6,14},{7,15},{8,0},{9,1},... | collective-permute-start | bytes 24584 | tf_op jit(solution)/shard_map/ppermute | solution.py:16
  128.5 129.2 %reduce-scatter.8.cloned.1.call-start = ((), (), s32[]{:S(2)}) async-start(), calls=%async_computation.5 | async-start | bytes 278528 | tf_op jit(solution)/shard_map/reduce_scatter | solution.py:86
  186.7 1.2 collective-permute-start.14
  187.8 3.7 %collective-permute-start.15 = (f32[16,128]{1,0:T(8,128)S(1)}, f32[16,128]{1,0:T(8,128)S(1)}, u32[]{:S(2)}, u32[]{:S(2)}) collective-permute-start(f32[16,128]{1,0:T(8,128)S(1)} %add.198), channel_id=1, source_target_pairs={{0,2},{1,3},{2,0},{3,1},{4,6},{5,7},{6,4},{7,5},{8,10},{9,11},{10,... | collective-permute-start | bytes 24584 | tf_op jit(solution)/shard_map/ppermute | solution.py:16
  191.5 4.9 %collective-permute-start.16 = (f32[16,128]{1,0:T(8,128)S(1)}, f32[16,128]{1,0:T(8,128)S(1)}, u32[]{:S(2)}, u32[]{:S(2)}) collective-permute-start(f32[16,128]{1,0:T(8,128)S(1)} %add.199), channel_id=1, source_target_pairs={{0,4},{1,5},{2,6},{3,7},{4,0},{5,1},{6,2},{7,3},{8,12},{9,13},{10,... | collective-permute-start | bytes 24584 | tf_op jit(solution)/shard_map/ppermute | solution.py:16
  192.1 14.2 %collective-permute-start.13 = (f32[19,1024]{1,0:T(8,128)S(1)}, f32[19,1024]{1,0:T(8,128)S(1)}, u32[]{:S(2)}, u32[]{:S(2)}) collective-permute-start(f32[19,1024]{1,0:T(8,128)S(1)} %pad_maximum_fusion.5), channel_id=1, source_target_pairs={{1,0},{2,1},{3,2},{4,3},{5,4},{6,5},{7,6},{8,7},{9,8},{10,9},{11,1... | collective-permute-start | bytes 233480 | tf_op jit(solution)/shard_map/ppermute | solution.py:29
  194.0 12.2 %collective-permute-start.12 = (f32[19,1024]{1,0:T(8,128)S(1)}, f32[19,1024]{1,0:T(8,128)S(1)}, u32[]{:S(2)}, u32[]{:S(2)}) collective-permute-start(f32[19,1024]{1,0:T(8,128)S(1)} %pad_maximum_fusion.5), channel_id=1, source_target_pairs={{0,1},{1,2},{2,3},{3,4},{4,5},{5,6},{6,7},{7,8},{8,9},{9,10},{10,1... | collective-permute-start | bytes 233480 | tf_op jit(solution)/shard_map/ppermute | solution.py:28
  196.5 5.0 %collective-permute-start.17 = (f32[16,128]{1,0:T(8,128)S(1)}, f32[16,128]{1,0:T(8,128)S(1)}, u32[]{:S(2)}, u32[]{:S(2)}) collective-permute-start(f32[16,128]{1,0:T(8,128)S(1)} %add.200), channel_id=1, source_target_pairs={{0,8},{1,9},{2,10},{3,11},{4,12},{5,13},{6,14},{7,15},{8,0},{9,1},... | collective-permute-start | bytes 24584 | tf_op jit(solution)/shard_map/ppermute | solution.py:16
Sparse Core Ops, SparseCore 0:
  55.2 56.6 reduce-scatter.3
  128.7 56.1 reduce-scatter.5
  201.6 56.0 reduce-scatter.7
